TPU v7x, 32 devices: a whole 2x2x4 slice. The times are simulated.
32 devices in a mesh: dp: 8 (over z, y), head: 4 (over x, core).
Axes of the slice: x: 2, y: 2, z: 4, core: 2. Of those that a mesh axis runs over, the one named last changes fastest.
Arguments:
- tokens: bfloat16 [32768, 512], P(('dp', 'head')), may hold values from -6 to 6
- segments: int32 [32768], P('dp'), may hold values from 0 to 255, never falling along the last dimension, each value on 1 to 256 neighbouring positions
- out_grad: bfloat16 [32768, 512], P(('dp', 'head')), may hold values from -6 to 6
- norm_params: float32 [4, 512], replicated, may hold values from -0.6 to 1.3
- norm_first: float32 [4, 512], replicated, may hold values from -0.0024414062 to 0.0024414062
- norm_second: float32 [4, 512], replicated, may hold values from 7.947286e-08 to 1.2715658e-06
- qkv_weight: float32 [512, 1536], P(None, 'head'), may hold values from -0.25 to 0.25
- qkv_moment: float32 [512, 1536], P(None, 'head'), may hold values from -0.0078125 to 0.0078125
- out_weight: float32 [512, 512], P('head'), may hold values from -2 to 2
- out_moment: float32 [512, 512], P('head'), may hold values from -0.0078125 to 0.0078125
- up_weight: float32 [512, 2048], P(None, ('dp', 'head')), may hold values from -0.25 to 0.25
- up_moment: float32 [512, 2048], P(None, ('dp', 'head')), may hold values from -0.0078125 to 0.0078125
- down_weight: float32 [512, 2048], P(None, ('dp', 'head')), may hold values from -0.125 to 0.125
- down_moment: float32 [512, 2048], P(None, ('dp', 'head')), may hold values from -0.0078125 to 0.0078125
Outputs:
- layer_out: bfloat16 [32768, 512], P(('dp', 'head'))
- input_grad: float32 [32768, 512], P(('dp', 'head'))
- grad_norm: float32 [], replicated
- clipped_grads: float32 [4, 512], replicated
- new_norm_first: float32 [4, 512], replicated
- new_norm_second: float32 [4, 512], replicated
- new_qkv_weight: float32 [512, 1536], P(None, 'head')
- new_qkv_moment: float32 [512, 1536], P(None, 'head')
- new_out_weight: float32 [512, 512], P('head')
- new_out_moment: float32 [512, 512], P('head')
- new_up_weight: float32 [512, 2048], P(None, ('dp', 'head'))
- new_up_moment: float32 [512, 2048], P(None, ('dp', 'head'))
- new_down_weight: float32 [512, 2048], P(None, ('dp', 'head'))
- new_down_moment: float32 [512, 2048], P(None, ('dp', 'head'))
Inputs may be any that keep to these rules, and one draw needn't show every extreme that they name: `segments`: segment ids never fall along the rows; each id covers 1 to 256 consecutive rows.
All inputs are finite; a program needn't handle non-finite values.
Results may differ from a plain program's by a relative error of at most 0.028.
Values may be sent and summed in bfloat16 or wider, within the bound.
A program may use at most 128 MiB of HBM per device.

v0:
```python
import math
import jax
import jax.numpy as jnp
from jax import lax
from jax.sharding import PartitionSpec as P

HEAD_DIM = 64
FF = 2048
SEQ = 512
NS_STEPS = 5
neg_fill = -1000000000.0
norm_eps = 1e-05
ns_a = 3.4445
ns_b = -4.775
ns_c = 2.0315
momentum_decay = 0.95
muon_rate = 0.5
muon_decay = 0.01
beta_one = 0.9
beta_two = 0.95


def normalize(values, gain, shift):
    mean = jnp.mean(values, axis=-1, keepdims=True)
    centered = values - mean
    factor = lax.rsqrt(jnp.mean(centered * centered, axis=-1, keepdims=True) + norm_eps)
    plain = centered * factor
    return (plain * gain + shift, plain, factor)


def normalize_back(upper, plain, factor, gain):
    inner = upper * gain
    lower = factor * (
        inner
        - jnp.mean(inner, axis=-1, keepdims=True)
        - plain * jnp.mean(inner * plain, axis=-1, keepdims=True)
    )
    return (lower, jnp.sum(upper * plain, axis=0), jnp.sum(upper, axis=0))


def masked_scores(query, keys, segment):
    scores = jnp.einsum(
        "qhd,khd->hqk", query, keys, preferred_element_type=jnp.float32
    ) * HEAD_DIM ** (-0.5)
    same = segment[:, None] == segment[None, :]
    return jnp.where(same[None], scores, neg_fill)


def attend_forward(block):
    query, keys, values, segment = block
    scores = masked_scores(query, keys, segment)
    top = jnp.max(scores, axis=-1, keepdims=True)
    weights = jnp.exp(scores - top)
    total = jnp.sum(weights, axis=-1, keepdims=True)
    probs = (weights / total).astype(jnp.bfloat16)
    context = jnp.einsum("hqk,khd->qhd", probs, values, preferred_element_type=jnp.float32)
    return (context.astype(jnp.bfloat16), top + jnp.log(total))


def attend_backward(block):
    query, keys, values, segment, context_grad, lse = block
    scores = masked_scores(query, keys, segment)
    probs = jnp.exp(scores - lse)
    probs_low = probs.astype(jnp.bfloat16)
    probs_grad = jnp.einsum(
        "qhd,khd->hqk", context_grad, values, preferred_element_type=jnp.float32
    )
    inner = jnp.sum(probs * probs_grad, axis=-1, keepdims=True)
    score_grad = (probs * (probs_grad - inner)).astype(jnp.bfloat16)
    query_grad = jnp.einsum(
        "hqk,khd->qhd", score_grad, keys, preferred_element_type=jnp.float32
    ) * HEAD_DIM ** (-0.5)
    key_grad = jnp.einsum(
        "hqk,qhd->khd", score_grad, query, preferred_element_type=jnp.float32
    ) * HEAD_DIM ** (-0.5)
    value_grad = jnp.einsum(
        "hqk,qhd->khd", probs_low, context_grad, preferred_element_type=jnp.float32
    )
    return jnp.stack([query_grad, key_grad, value_grad], axis=2).astype(jnp.bfloat16)


def gram_left(block):
    return lax.dot_general(
        block, block, (((1,), (1,)), ((), ())), preferred_element_type=jnp.float32
    )


def gram_right(block):
    return lax.dot_general(
        block, block, (((0,), (0,)), ((), ())), preferred_element_type=jnp.float32
    )


def squares_of(moment, grad, weight):
    return (
        jnp.stack([jnp.sum(moment * moment), jnp.sum(moment * grad), jnp.sum(grad * grad)]) * weight
    )


def shards(
    tokens,
    segments,
    out_grad,
    norm_params,
    norm_first,
    norm_second,
    qkv_weight,
    qkv_moment,
    out_weight,
    out_moment,
    up_weight,
    up_moment,
    down_weight,
    down_moment,
):
    width = tokens.shape[1]
    group = segments.shape[0]
    narrow = out_weight.shape[0]
    heads_here = narrow // HEAD_DIM
    sequences = group // SEQ
    inputs = tokens.astype(jnp.float32)
    first, first_plain, first_factor = normalize(inputs, norm_params[0], norm_params[1])
    first_all = lax.all_gather(first.astype(jnp.bfloat16), "head", axis=0, tiled=True)
    qkv_low = qkv_weight.astype(jnp.bfloat16)
    out_low = out_weight.astype(jnp.bfloat16)
    mixed = jnp.dot(first_all, qkv_low, preferred_element_type=jnp.float32).astype(jnp.bfloat16)
    mixed = mixed.reshape(sequences, SEQ, heads_here, 3, HEAD_DIM)
    segment_rows = segments.reshape(sequences, SEQ)
    query = mixed[:, :, :, 0]
    keys = mixed[:, :, :, 1]
    values = mixed[:, :, :, 2]
    context, lse = lax.map(attend_forward, (query, keys, values, segment_rows))
    context = context.reshape(group, narrow)
    context_rows = lax.all_to_all(context, "head", split_axis=0, concat_axis=1, tiled=True)
    out_full = lax.all_gather(out_low, "head", axis=0, tiled=True)
    attended = jnp.dot(context_rows, out_full, preferred_element_type=jnp.float32)
    middle = inputs + attended
    second, second_plain, second_factor = normalize(middle, norm_params[2], norm_params[3])
    second_low = second.astype(jnp.bfloat16)
    up_all, down_all = (
        lax.all_gather(up_weight.astype(jnp.bfloat16), ("dp", "head"), axis=1, tiled=True),
        lax.all_gather(down_weight.astype(jnp.bfloat16), ("dp", "head"), axis=1, tiled=True),
    )
    hidden = jnp.dot(second_low, up_all, preferred_element_type=jnp.float32)
    switch = jax.nn.sigmoid(1.702 * hidden)
    active = (hidden * switch).astype(jnp.bfloat16)
    result = middle + lax.dot_general(
        active, down_all, (((1,), (1,)), ((), ())), preferred_element_type=jnp.float32
    )
    layer_out = result.astype(jnp.bfloat16)
    down_grad = lax.dot_general(
        out_grad, active, (((0,), (0,)), ((), ())), preferred_element_type=jnp.float32
    )
    active_grad = jnp.dot(out_grad, down_all, preferred_element_type=jnp.float32)
    hidden_grad = (active_grad * (switch + 1.702 * hidden * switch * (1.0 - switch))).astype(
        jnp.bfloat16
    )
    up_grad = lax.dot_general(
        second_low, hidden_grad, (((0,), (0,)), ((), ())), preferred_element_type=jnp.float32
    )
    second_grad = lax.dot_general(
        hidden_grad, up_all, (((1,), (1,)), ((), ())), preferred_element_type=jnp.float32
    )
    up_part, down_part = (
        lax.psum_scatter(up_grad, ("dp", "head"), scatter_dimension=1, tiled=True),
        lax.psum_scatter(down_grad, ("dp", "head"), scatter_dimension=1, tiled=True),
    )
    middle_lower, gain_two, shift_two = normalize_back(
        second_grad, second_plain, second_factor, norm_params[2]
    )
    middle_grad = out_grad.astype(jnp.float32) + middle_lower
    attended_low = middle_grad.astype(jnp.bfloat16)
    rows_grad = lax.dot_general(
        attended_low, out_full, (((1,), (1,)), ((), ())), preferred_element_type=jnp.float32
    ).astype(jnp.bfloat16)
    context_grad = lax.all_to_all(rows_grad, "head", split_axis=1, concat_axis=0, tiled=True)
    whole_out = lax.dot_general(
        context_rows, attended_low, (((0,), (0,)), ((), ())), preferred_element_type=jnp.float32
    )
    out_part = lax.psum_scatter(
        whole_out.astype(jnp.bfloat16), "head", scatter_dimension=0, tiled=True
    )
    context_grad = context_grad.reshape(sequences, SEQ, heads_here, HEAD_DIM)
    mixed_grad = lax.map(attend_backward, (query, keys, values, segment_rows, context_grad, lse))
    mixed_grad = mixed_grad.reshape(group, 3 * narrow)
    qkv_part = lax.dot_general(
        first_all, mixed_grad, (((0,), (0,)), ((), ())), preferred_element_type=jnp.float32
    )
    mixed_rows = lax.all_to_all(mixed_grad, "head", split_axis=0, concat_axis=1, tiled=True)
    qkv_full = lax.all_gather(qkv_low, "head", axis=1, tiled=True)
    first_grad = lax.dot_general(
        mixed_rows, qkv_full, (((1,), (1,)), ((), ())), preferred_element_type=jnp.float32
    )
    input_lower, gain_one, shift_one = normalize_back(
        first_grad, first_plain, first_factor, norm_params[0]
    )
    input_grad = middle_grad + input_lower
    qkv_sum, out_sum = (
        lax.psum(qkv_part.astype(jnp.bfloat16), "dp").astype(jnp.float32),
        lax.psum(out_part, "dp").astype(jnp.float32),
    )
    leading = (lax.axis_index("dp") == 0).astype(jnp.float32)
    moments = [qkv_moment, out_moment, up_moment, down_moment]
    grads = [qkv_sum, out_sum, up_part, down_part]
    stats = jnp.stack(
        [
            squares_of(qkv_moment, qkv_sum, leading),
            squares_of(out_moment, out_sum, leading),
            squares_of(up_moment, up_part, 1.0),
            squares_of(down_moment, down_part, 1.0),
        ]
    )
    vector_part = jnp.stack([gain_one, shift_one, gain_two, shift_two])
    vector_sum, stat_sum = lax.psum((vector_part, stats), ("dp", "head"))
    grad_norm = jnp.sqrt(jnp.sum(stat_sum[:, 2]) + jnp.sum(vector_sum * vector_sum))
    clip = jnp.minimum(1.0, 1.0 / (grad_norm + 1e-06))
    sizes = jnp.sqrt(
        momentum_decay * momentum_decay * stat_sum[:, 0]
        + 2.0 * momentum_decay * clip * stat_sum[:, 1]
        + clip * clip * stat_sum[:, 2]
    )
    new_moments = [momentum_decay * moments[index] + clip * grads[index] for index in range(4)]
    starts = [
        (new_moments[index] / (sizes[index] + 1e-07)).astype(jnp.bfloat16) for index in range(4)
    ]
    up_block, down_block = (
        lax.all_gather(starts[2], "dp", axis=1, tiled=True),
        lax.all_gather(starts[3], "dp", axis=1, tiled=True),
    )
    blocks = [starts[0], starts[1], up_block, down_block]
    for turn in range(NS_STEPS):
        partials = (
            gram_left(blocks[0]),
            gram_right(blocks[1]),
            gram_left(blocks[2]),
            gram_left(blocks[3]),
        )
        grams = (
            lax.psum(partials[0].astype(jnp.bfloat16), "head").astype(jnp.float32),
            lax.psum(partials[1].astype(jnp.bfloat16), "head").astype(jnp.float32),
            lax.psum(partials[2].astype(jnp.bfloat16), "head").astype(jnp.float32),
            lax.psum(partials[3].astype(jnp.bfloat16), "head").astype(jnp.float32),
        )
        updated = []
        for index in range(4):
            gram = grams[index].astype(jnp.bfloat16)
            mix = (
                ns_b * gram.astype(jnp.float32)
                + ns_c * jnp.dot(gram, gram, preferred_element_type=jnp.float32)
            ).astype(jnp.bfloat16)
            if index == 1:
                product = jnp.dot(blocks[index], mix, preferred_element_type=jnp.float32)
            else:
                product = jnp.dot(mix, blocks[index], preferred_element_type=jnp.float32)
            updated.append(
                (ns_a * blocks[index].astype(jnp.float32) + product).astype(jnp.bfloat16)
            )
        blocks = updated
    share = up_weight.shape[1]
    offset = lax.axis_index("dp") * share
    owned = [
        blocks[0],
        blocks[1],
        lax.dynamic_slice_in_dim(blocks[2], offset, share, 1),
        lax.dynamic_slice_in_dim(blocks[3], offset, share, 1),
    ]
    weights = [qkv_weight, out_weight, up_weight, down_weight]
    factors = [
        math.sqrt(3.0),
        math.sqrt(SEQ / 8.0),
        math.sqrt(max(1.0, FF / width)),
        math.sqrt(max(1.0, FF / width)),
    ]
    new_weights = [
        weights[index] * (1.0 - muon_rate * muon_decay)
        - muon_rate * factors[index] * owned[index].astype(jnp.float32)
        for index in range(4)
    ]
    clipped = clip * vector_sum
    first_new = beta_one * norm_first + (1.0 - beta_one) * clipped
    second_new = beta_two * norm_second + (1.0 - beta_two) * clipped * clipped
    return (
        layer_out,
        input_grad,
        grad_norm,
        clipped,
        first_new,
        second_new,
        new_weights[0],
        new_moments[0],
        new_weights[1],
        new_moments[1],
        new_weights[2],
        new_moments[2],
        new_weights[3],
        new_moments[3],
    )


def solution(mesh):
    placed = (
        P(("dp", "head"), None),
        P("dp"),
        P(("dp", "head"), None),
        P(),
        P(),
        P(),
        P(None, "head"),
        P(None, "head"),
        P("head", None),
        P("head", None),
        P(None, ("dp", "head")),
        P(None, ("dp", "head")),
        P(None, ("dp", "head")),
        P(None, ("dp", "head")),
    )
    return jax.shard_map(
        shards,
        mesh=mesh,
        in_specs=placed,
        out_specs=(
            P(("dp", "head"), None),
            P(("dp", "head"), None),
            P(),
            P(),
            P(),
            P(),
            P(None, "head"),
            P(None, "head"),
            P("head", None),
            P("head", None),
            P(None, ("dp", "head")),
            P(None, ("dp", "head")),
            P(None, ("dp", "head")),
            P(None, ("dp", "head")),
        ),
        check_vma=False,
    )
```

profile of v0, /device:TPU:0, one launch (start us, length us, event | category | flops | bytes accessed | tf_op | source)
XLA Modules:
  0.0 1169.6 jit_solution(14758495943311568836)
XLA Ops:
  13.5 35.1 %all-gather.5.cloned.1.call-done = bf16[4096,512]{0,1:T(8,128)(2,1)} async-done(((bf16[1024,512]{0,1:T(8,128)(2,1)}), bf16[4096,512]{0,1:T(8,128)(2,1)}) %all-gather.5.cloned.1.call-update) | async-done | bytes 4194320 | tf_op jit(solution)/shard_map/all_gather | solution.py:123
  48.6 6.2 convolution_convert_fusion.2
  54.8 4.8 copy.76
  59.6 3.3 copy.103
  65.1 40.1 %while.22 = (s32[]{:T(128)}, bf16[8,512,2,64]{1,3,2,0:T(8,128)(2,1)}, f32[8,2,512,1]{2,1,3,0:T(2,128)}, bf16[8,512,2,64]{1,3,2,0:T(8,128)(2,1)}, s32[8,512]{1,0:...) while((s32[]{:T(128)}, ...), condition=%wide.region_5.6_spmd, body=%wide.region_2.5_spmd.sunk | while | flops 140835840 | bytes 7905881 | solution.py:132
  105.2 3.5 copy.80
  113.8 3.6 all-to-all-start
  118.9 17.6 %all_gather.22 = bf16[512,512]{1,0:T(8,128)(2,1)} all-gather(bf16[128,512]{1,0:T(8,128)(2,1)S(1)} %convert_element_type.448), channel_id=1, replica_groups=mesh['dp'=8,'head'=4] {'head'}, dimensions={0}, use_global_device_ids=true | all-gather | bytes 655360 | tf_op jit(solution)/shard_map/all_gather | solution.py:135
  140.3 8.4 multiply_convert_fusion.2
  148.7 18.5 %all-gather.9.cloned.1.call-done = bf16[512,2048]{0,1:T(8,128)(2,1)} async-done(((bf16[512,64]{0,1:T(8,128)(2,1)}), bf16[512,2048]{0,1:T(8,128)(2,1)}) %all-gather.9.cloned.1.call-update) | async-done | bytes 2097168 | tf_op jit(solution)/shard_map/all_gather | solution.py:142
  167.2 8.4 multiply_convert_fusion.1
  175.7 4.2 fusion.268
  182.8 3.0 multiply_reduce_fusion.1
  190.0 4.2 all-to-all-start.1
  197.5 11.2 all-to-all-done.1
  216.4 81.9 %while.23 = (s32[]{:T(128)}, bf16[8,512,2,3,64]{1,4,2,3,0:T(8,128)(2,1)}, bf16[8,512,2,64]{1,3,2,0:T(8,128)(2,1)}, s32[8,512]{1,0:T(8,128)}, bf16[8,512,2,64]{1,...) while((s32[]{:T(128)}, ...), condition=%wide.region_12.13_spmd, body=%wide.region_10.12_spmd.sunk | while | flops 342031360 | bytes 18380900 | solution.py:184
  298.4 3.7 copy.90
  305.4 3.1 convolution_convert_fusion.25
  309.2 7.3 fusion.263
  316.7 6.9 convolution_bitcast_fusion
  323.6 6.0 all_to_all.47
  329.7 4.6 copy.91
  334.2 4.8 all-to-all-start.2
  339.1 41.0 %all-reduce.14.cloned.1.call-done = (bf16[128,512]{1,0:T(8,128)(2,1)}, bf16[512,384]{1,0:T(8,128)(2,1)}) async-done(((bf16[128,512]{1,0:T(8,128)(2,1)}, bf16[512,384]{1,0:T(8,128)(2,1)}), (bf16[128,512]{1,0:T(8,128)(2,1)}, bf16[512,384]{1,0:T(8,128)(2,1)})) %all-reduce.14.cloned.1.call-update) | async-done | bytes 524304 | tf_op jit(solution)/shard_map/psum | solution.py:200
  388.8 12.2 %all-gather.11.cloned.1.call-done = bf16[512,1536]{1,0:T(8,128)(2,1)} async-done(((bf16[512,384]{1,0:T(8,128)(2,1)}), bf16[512,1536]{1,0:T(8,128)(2,1)}) %all-gather.11.cloned.1.call-update) | async-done | bytes 1572880 | tf_op jit(solution)/shard_map/all_gather | solution.py:190
  401.0 6.1 fusion.269
  413.6 130.7 %reduce-scatter.6.cloned.1.call-done = f32[512,64]{0,1:T(8,128)} async-done(((f32[512,2048]{0,1:T(8,128)}), f32[512,64]{0,1:T(8,128)}) %reduce-scatter.6.cloned.1.call-update) | async-done | bytes 131088 | tf_op jit(solution)/shard_map/reduce_scatter | solution.py:165
  545.9 137.6 %reduce-scatter.8.cloned.1.call-done = f32[512,64]{0,1:T(8,128)} async-done(((f32[512,2048]{0,1:T(8,128)}), f32[512,64]{0,1:T(8,128)}) %reduce-scatter.8.cloned.1.call-update) | async-done | bytes 131088 | tf_op jit(solution)/shard_map/reduce_scatter | solution.py:166
  685.2 4.0 maximum_bitcast_fusion
  690.4 37.2 %all-reduce = (f32[4,3]{1,0:T(4,128)S(1)}, f32[4,512]{1,0:T(4,128)}) all-reduce(f32[4,3]{1,0:T(4,128)} %pad_maximum_fusion.1, f32[4,512]{1,0:T(4,128)} %pad_maximum_fusion), channel_id=1, replica_groups=mesh['dp'=8,'head'=4] {'dp','head'}, use_global_device_ids=true, to_apply=%region_32.33 | all-reduce | flops 2060 | bytes 16480 | tf_op jit(solution)/shard_map/psum | solution.py:214
  737.7 31.5 %all_gather.27 = bf16[512,512]{0,1:T(8,128)(2,1)S(1)} all-gather(bf16[512,64]{0,1:T(8,128)(2,1)S(1)} %get-tuple-element.241), channel_id=1, replica_groups=mesh['dp'=8,'head'=4] {'dp'}, dimensions={1}, use_global_device_ids=true | all-gather | bytes 589824 | tf_op jit(solution)/shard_map/all_gather | solution.py:228
  772.0 31.2 %all_gather.26 = bf16[512,512]{0,1:T(8,128)(2,1)S(1)} all-gather(bf16[512,64]{0,1:T(8,128)(2,1)S(1)} %get-tuple-element.243), channel_id=1, replica_groups=mesh['dp'=8,'head'=4] {'dp'}, dimensions={1}, use_global_device_ids=true | all-gather | bytes 589824 | tf_op jit(solution)/shard_map/all_gather | solution.py:227
  808.4 51.9 %all-reduce.24.cloned.1.call-done = (bf16[512,512]{1,0:T(8,128)(2,1)}, bf16[512,512]{1,0:T(8,128)(2,1)}, bf16[512,512]{1,0:T(8,128)(2,1)}, bf16[512,512]{1,0:T(8,128)(2,1)}) async-done(((bf16[512,512]{1,0:T(8,128)(2,1)}, bf16[512,512]{1,0:T(8,128)(2,1)}, bf16[512,512]{1,0:T(8,128)(2,1)}, bf16[512,512]{1,0:T(8,128)(2,1)}), (bf16[512,512]{1,0:T(8,128)(2,1)}, bf16[512,512]{1,0:T(8,128)(2,1)}, ...) | async-done | bytes 2097168 | tf_op jit(solution)/shard_map/psum | solution.py:239
  860.3 3.5 fusion.100
  866.2 3.5 fusion.96
  879.5 52.1 %all-reduce.22.cloned.1.call-done = (bf16[512,512]{1,0:T(8,128)(2,1)}, bf16[512,512]{1,0:T(8,128)(2,1)}, bf16[512,512]{1,0:T(8,128)(2,1)}, bf16[512,512]{1,0:T(8,128)(2,1)}) async-done(((bf16[512,512]{1,0:T(8,128)(2,1)}, bf16[512,512]{1,0:T(8,128)(2,1)}, bf16[512,512]{1,0:T(8,128)(2,1)}, bf16[512,512]{1,0:T(8,128)(2,1)}), (bf16[512,512]{1,0:T(8,128)(2,1)}, bf16[512,512]{1,0:T(8,128)(2,1)}, ...) | async-done | bytes 2097168 | tf_op jit(solution)/shard_map/psum | solution.py:239
  931.6 3.5 fusion.101
  937.6 3.5 fusion.97
  953.8 52.1 %all-reduce.20.cloned.1.call-done = (bf16[512,512]{1,0:T(8,128)(2,1)}, bf16[512,512]{1,0:T(8,128)(2,1)}, bf16[512,512]{1,0:T(8,128)(2,1)}, bf16[512,512]{1,0:T(8,128)(2,1)}) async-done(((bf16[512,512]{1,0:T(8,128)(2,1)}, bf16[512,512]{1,0:T(8,128)(2,1)}, bf16[512,512]{1,0:T(8,128)(2,1)}, bf16[512,512]{1,0:T(8,128)(2,1)}), (bf16[512,512]{1,0:T(8,128)(2,1)}, bf16[512,512]{1,0:T(8,128)(2,1)}, ...) | async-done | bytes 2097168 | tf_op jit(solution)/shard_map/psum | solution.py:239
  1006.0 3.4 fusion.102
  1011.8 3.5 fusion.98
  1025.1 6.8 add_convert_fusion
  1034.8 42.2 %all-reduce.18.cloned.1.call-done = (bf16[512,512]{1,0:T(8,128)(2,1)}, bf16[512,512]{1,0:T(8,128)(2,1)}, bf16[512,512]{1,0:T(8,128)(2,1)}, bf16[512,512]{1,0:T(8,128)(2,1)}) async-done(((bf16[512,512]{1,0:T(8,128)(2,1)}, bf16[512,512]{1,0:T(8,128)(2,1)}, bf16[512,512]{1,0:T(8,128)(2,1)}, bf16[512,512]{1,0:T(8,128)(2,1)}), (bf16[512,512]{1,0:T(8,128)(2,1)}, bf16[512,512]{1,0:T(8,128)(2,1)}, ...) | async-done | bytes 2097168 | tf_op jit(solution)/shard_map/psum | solution.py:239
  1077.0 3.5 fusion.103
  1083.0 3.4 fusion.99
  1096.0 3.6 fusion.53
  1103.8 44.4 %all-reduce.16.cloned.1.call-done = (bf16[512,512]{1,0:T(8,128)(2,1)}, bf16[512,512]{1,0:T(8,128)(2,1)}, bf16[512,512]{1,0:T(8,128)(2,1)}, bf16[512,512]{1,0:T(8,128)(2,1)}) async-done(((bf16[512,512]{1,0:T(8,128)(2,1)}, bf16[512,512]{1,0:T(8,128)(2,1)}, bf16[512,512]{1,0:T(8,128)(2,1)}, bf16[512,512]{1,0:T(8,128)(2,1)}), (bf16[512,512]{1,0:T(8,128)(2,1)}, bf16[512,512]{1,0:T(8,128)(2,1)}, ...) | async-done | bytes 2097168 | tf_op jit(solution)/shard_map/psum | solution.py:239
  1148.2 3.2 fusion.112
  (354 shorter events, 264.9 us)
Async XLA Ops:
  7.2 41.4 %all-gather.5.cloned.1.call-start = ((), (), s32[]{:S(2)}) async-start(), calls=%async_computation.6 | async-start | bytes 5242880 | tf_op jit(solution)/shard_map/all_gather | solution.py:123
  8.9 3.1 copy-start.26
  9.3 3.5 copy-start.13
  11.3 128.7 %all-gather.7.cloned.1.call-start = ((), (), s32[]{:S(2)}) async-start(), calls=%async_computation.7 | async-start | bytes 2162688 | tf_op jit(solution)/shard_map/all_gather | solution.py:141
  12.0 155.2 %all-gather.9.cloned.1.call-start = ((), (), s32[]{:S(2)}) async-start(), calls=%async_computation.8 | async-start | bytes 2162688 | tf_op jit(solution)/shard_map/all_gather | solution.py:142
  12.8 42.0 %copy-start.10 = (bf16[512,384]{1,0:T(8,128)(2,1)}, bf16[512,384]{1,0:T(8,128)(2,1)S(1)}, u32[]{:S(2)}) copy-start(bf16[512,384]{1,0:T(8,128)(2,1)S(1)} %convert_element_type.446) | copy-start | bytes 1179652
  105.2 6.1 copy-start.4
  105.2 6.1 copy-start.5
  111.2 6.2 copy-start.30
  113.8 3.7 copy-start.11
  113.8 22.7 %all-to-all-start = ((bf16[4,1024,128]{1,2,0:T(8,128)(2,1)}), bf16[4,1024,128]{1,2,0:T(8,128)(2,1)S(1)}, u32[]{:S(2)}, u32[]{:S(2)}) async-start(bf16[4,1024,128]{1,2,0:T(8,128)(2,1)} %copy.81), calls=%async_computation | async-start | bytes 2097152 | tf_op jit(solution)/shard_map/all_to_all | solution.py:134
  139.6 43.2 %copy-start = (f32[1024,512]{0,1:T(8,128)}, f32[1024,512]{0,1:T(8,128)S(1)}, u32[]{:S(2)}) copy-start(f32[1024,512]{0,1:T(8,128)S(1)} %get-tuple-element.263) | copy-start | bytes 6291460
  167.2 8.4 copy-start.49
  175.7 4.2 copy-start.51
  182.8 3.0 copy-start.7
  190.0 18.8 %all-to-all-start.1 = ((bf16[1024,4,128]{0,2,1:T(8,128)(2,1)}), bf16[1024,4,128]{0,2,1:T(8,128)(2,1)}, u32[]{:S(2)}, u32[]{:S(2)}) async-start(bf16[1024,4,128]{0,2,1:T(8,128)(2,1)} %bitcast.284), calls=%async_computation.1 | async-start | bytes 2097152 | tf_op jit(solution)/shard_map/all_to_all | solution.py:176
  194.2 114.3 %reduce-scatter.4.cloned.1.call-start = ((), (), s32[]{:S(2)}) async-start(), calls=%async_computation.10 | async-start | bytes 655360 | tf_op jit(solution)/shard_map/reduce_scatter | solution.py:180
  197.1 183.1 %all-reduce.14.cloned.1.call-start = ((), (), s32[]{:S(2)}) async-start(), calls=%async_computation.13 | async-start | bytes 1048576 | tf_op jit(solution)/shard_map/psum | solution.py:200
  302.1 3.3 copy-start.48
  308.6 92.4 %all-gather.11.cloned.1.call-start = ((), (), s32[]{:S(2)}) async-start(), calls=%async_computation.9 | async-start | bytes 1966080 | tf_op jit(solution)/shard_map/all_gather | solution.py:190
  309.1 235.2 %reduce-scatter.6.cloned.1.call-start = ((), (), s32[]{:S(2)}) async-start(), calls=%async_computation.11 | async-start | bytes 4325376 | tf_op jit(solution)/shard_map/reduce_scatter | solution.py:165
  316.5 367.0 %reduce-scatter.8.cloned.1.call-start = ((), (), s32[]{:S(2)}) async-start(), calls=%async_computation.12 | async-start | bytes 4325376 | tf_op jit(solution)/shard_map/reduce_scatter | solution.py:166
  334.2 50.5 %copy-start.12 = (f32[128,512]{1,0:T(8,128)S(1)}, f32[128,512]{1,0:T(8,128)}, u32[]{:S(2)}) copy-start(f32[128,512]{1,0:T(8,128)} %param.27) | copy-start | bytes 786436
  334.2 66.8 %all-to-all-start.2 = ((bf16[4,1024,384]{1,2,0:T(8,128)(2,1)}), bf16[4,1024,384]{1,2,0:T(8,128)(2,1)}, u32[]{:S(2)}, u32[]{:S(2)}) async-start(bf16[4,1024,384]{1,2,0:T(8,128)(2,1)} %copy.91), calls=%async_computation.2 | async-start | bytes 6291456 | tf_op jit(solution)/shard_map/all_to_all | solution.py:189
  339.1 521.2 %all-reduce.24.cloned.1.call-start = ((), (), s32[]{:S(2)}) async-start(), calls=%async_computation.18 | async-start | bytes 4194304 | tf_op jit(solution)/shard_map/psum | solution.py:239
  410.0 322.7 %copy-start.8 = (bf16[512,384]{1,0:T(8,128)(2,1)S(1)}, bf16[512,384]{1,0:T(8,128)(2,1)}, u32[]{:S(2)}) copy-start(bf16[512,384]{1,0:T(8,128)(2,1)} %get-tuple-element.220) | copy-start | bytes 1179652
  734.8 36.5 %copy-start.22 = (f32[512,64]{0,1:T(8,128)S(1)}, f32[512,64]{0,1:T(8,128)}, u32[]{:S(2)}) copy-start(f32[512,64]{0,1:T(8,128)} %param.29) | copy-start | bytes 393220
  734.8 36.5 %copy-start.23 = (f32[512,64]{0,1:T(8,128)S(1)}, f32[512,64]{0,1:T(8,128)}, u32[]{:S(2)}) copy-start(f32[512,64]{0,1:T(8,128)} %reduce-scatter.6.cloned.1.call-done) | copy-start | bytes 393220
  769.3 35.2 %copy-start.24 = (bf16[512,512]{0,1:T(8,128)(2,1)}, bf16[512,512]{0,1:T(8,128)(2,1)S(1)}, u32[]{:S(2)}) copy-start(bf16[512,512]{0,1:T(8,128)(2,1)S(1)} %all_gather.27) | copy-start | bytes 1572868
  769.3 36.5 %copy-start.32 = (f32[128,512]{1,0:T(8,128)S(1)}, f32[128,512]{1,0:T(8,128)}, u32[]{:S(2)}) copy-start(f32[128,512]{1,0:T(8,128)} %fusion.219) | copy-start | bytes 786436
  770.5 36.3 %copy-start.15 = (f32[512,384]{1,0:T(8,128)S(1)}, f32[512,384]{1,0:T(8,128)}, u32[]{:S(2)}) copy-start(f32[512,384]{1,0:T(8,128)} %fusion.174) | copy-start | bytes 2359300
  808.2 123.5 %all-reduce.22.cloned.1.call-start = ((), (), s32[]{:S(2)}) async-start(), calls=%async_computation.17 | async-start | bytes 4194304 | tf_op jit(solution)/shard_map/psum | solution.py:239
  866.2 6.0 copy-start.33
  879.5 126.5 %all-reduce.20.cloned.1.call-start = ((), (), s32[]{:S(2)}) async-start(), calls=%async_computation.16 | async-start | bytes 4194304 | tf_op jit(solution)/shard_map/psum | solution.py:239
  953.8 123.2 %all-reduce.18.cloned.1.call-start = ((), (), s32[]{:S(2)}) async-start(), calls=%async_computation.15 | async-start | bytes 4194304 | tf_op jit(solution)/shard_map/psum | solution.py:239
  1011.8 6.0 copy-start.21
  1023.5 8.4 copy-start.9
  1024.8 123.3 %all-reduce.16.cloned.1.call-start = ((), (), s32[]{:S(2)}) async-start(), calls=%async_computation.14 | async-start | bytes 4194304 | tf_op jit(solution)/shard_map/psum | solution.py:239
  1083.0 5.9 copy-start.19
  1099.6 3.6 copy-start.40
  1099.6 48.6 %copy-start.42 = (bf16[512,512]{0,1:T(8,128)(2,1)S(1)}, bf16[512,512]{0,1:T(8,128)(2,1)}, u32[]{:S(2)}) copy-start(bf16[512,512]{0,1:T(8,128)(2,1)} %fusion.103) | copy-start | bytes 1572868
  1102.6 48.8 %copy-start.43 = (bf16[512,512]{0,1:T(8,128)(2,1)S(1)}, bf16[512,512]{0,1:T(8,128)(2,1)}, u32[]{:S(2)}) copy-start(bf16[512,512]{0,1:T(8,128)(2,1)} %fusion.99) | copy-start | bytes 1572868
  1103.2 50.5 %copy-start.34 = (f32[4,512]{1,0:T(4,128)}, f32[4,512]{1,0:T(4,128)S(1)}, u32[]{:S(2)}) copy-start(f32[4,512]{1,0:T(4,128)S(1)} %get-tuple-element.246) | copy-start | bytes 24580
  1151.4 4.0 copy-start.29
  1151.4 5.6 copy-start.17
  1151.4 5.6 copy-start.31
  1153.7 6.1 copy-start.14
  1155.4 4.4 copy-start.50
  (20 other events, 42.1 us)
Sparse Core Ops, SparseCore 0:
  11.4 37.1 all-gather.4
  52.0 56.3 all-gather.6
  111.9 55.3 all-gather.8
  197.8 21.8 reduce-scatter.3
  308.7 71.3 all-reduce.13
  382.1 18.8 all-gather.10
  403.3 140.9 reduce-scatter.5
  546.6 136.9 reduce-scatter.7
  808.3 51.9 all-reduce.23
  879.6 51.9 all-reduce.21
  953.9 52.0 all-reduce.19
  1025.0 51.9 all-reduce.17
  1096.1 52.0 all-reduce.15
where the time goes:
time: 1180 us; the launch traced here: 1170 us
  waiting for transfers between devices  630 us (53%)
  matrix products  239 us (20%)
  blocking collectives  118 us (10%)
  local copies, waits for them, and re-layouts  78.6 us (7%)
  other arithmetic  69.6 us (6%)
  between operations  20.1 us (2%)
  starting transfers between devices  14.3 us (1%)
    psum x5, waiting for transfers between devices, shards(): lax.psum(partials[0].astype(jnp.bfloat16), 'head').astype(jnp.float32)  243 us
    reduce_scatter x1, waiting for transfers between devices, shards(): lax.psum_scatter(down_grad, ('dp', 'head'), scatter_dimension=1, tiled=True)  138 us
    reduce_scatter x1, waiting for transfers between devices, shards(): lax.psum_scatter(up_grad, ('dp', 'head'), scatter_dimension=1, tiled=True)  131 us
    dot_general x15, matrix products, shards(): product = jnp.dot(mix, blocks[index], preferred_element_type=jnp.float32)  45.7 us
    psum x1, waiting for transfers between devices, shards(): lax.psum(out_part, 'dp').astype(jnp.float32)  41 us
    psum x1, blocking collectives, shards(): vector_sum, stat_sum = lax.psum((vector_part, stats), ('dp', 'head'))  37.2 us
    all_gather x1, waiting for transfers between devices, shards(): lax.all_gather(first.astype(jnp.bfloat16), 'head', axis=0, tiled=True)  35.1 us
    all_gather x1, blocking collectives, shards(): lax.all_gather(starts[3], 'dp', axis=1, tiled=True)  31.5 us
  transfers between devices with their start and end apart: 16, of which 12 were waited for; matrix products, arithmetic and copies ran while one was open for 20% of the time, Pallas kernels for 0%

commit v1 on v0

--- a/solution.py
+++ b/solution.py
@@ -18,6 +18,28 @@
 muon_decay = 0.01
 beta_one = 0.9
 beta_two = 0.95
+
+
+def in_order(blocks, dim):
+    lengths = list(blocks.shape[1:])
+    lengths[dim] *= blocks.shape[0]
+    return jnp.moveaxis(blocks, 0, dim).reshape(lengths)
+
+
+def collect(x, axis, dim):
+    count = lax.axis_size(axis)
+    pairs = [(i, (i + 1) % count) for i in range(count)]
+    back = [(b, a) for a, b in pairs]
+    lower, upper = ([], [])
+    for step in range(count - 1):
+        if step % 2 == 0:
+            lower.append(lax.ppermute(lower[-1] if lower else x, axis, pairs))
+        else:
+            upper.append(lax.ppermute(upper[-1] if upper else x, axis, back))
+    blocks = jnp.stack([*lower[::-1], x, *upper])
+    shift = lax.axis_index(axis) - len(lower)
+    blocks = blocks[(jnp.arange(count) - shift) % count]
+    return in_order(blocks, dim)
 
 
 def normalize(values, gain, shift):
@@ -225,7 +247,7 @@
     ]
     up_block, down_block = (
         lax.all_gather(starts[2], "dp", axis=1, tiled=True),
-        lax.all_gather(starts[3], "dp", axis=1, tiled=True),
+        collect(starts[3], "dp", 1),
     )
     blocks = [starts[0], starts[1], up_block, down_block]
     for turn in range(NS_STEPS):

time: 1180 us -> 1180 us (level)
  blocking collectives: 118 us -> 86 us
  starting transfers between devices: 14.3 us -> 28.6 us
    all_gather x1 -> x0, blocking collectives: 31.5 us -> none  [shards(): lax.all_gather(starts[3], 'dp', axis=1, tiled=True)]
    ppermute x0 -> x7, starting transfers between devices: none -> 14.3 us  [the longest x3 11.6 us: collect(): upper.append(lax.ppermute(upper[-1] if upper else x, axis, back))]
  transfers between devices with their start and end apart: 16 -> 23, of which waited for: 12 -> 15; matrix products, arithmetic and copies ran while one was open for 20% -> 21% of each run, Pallas kernels for 0% -> 0%
where the time goes in v1:
time: 1180 us; the launch traced here: 1170 us
  waiting for transfers between devices  637 us (54%)
  matrix products  240 us (20%)
  local copies, waits for them, and re-layouts  87 us (7%)
  blocking collectives  86 us (7%)
  other arithmetic  68.8 us (6%)
  starting transfers between devices  28.6 us (2%)
  between operations  20.2 us (2%)
    psum x5, waiting for transfers between devices, shards(): lax.psum(partials[0].astype(jnp.bfloat16), 'head').astype(jnp.float32)  242 us
    reduce_scatter x1, waiting for transfers between devices, shards(): lax.psum_scatter(down_grad, ('dp', 'head'), scatter_dimension=1, tiled=True)  138 us
    reduce_scatter x1, waiting for transfers between devices, shards(): lax.psum_scatter(up_grad, ('dp', 'head'), scatter_dimension=1, tiled=True)  131 us
    dot_general x15, matrix products, shards(): product = jnp.dot(mix, blocks[index], preferred_element_type=jnp.float32)  45.7 us
    psum x1, waiting for transfers between devices, shards(): lax.psum(out_part, 'dp').astype(jnp.float32)  40.4 us
    psum x1, blocking collectives, shards(): vector_sum, stat_sum = lax.psum((vector_part, stats), ('dp', 'head'))  37.2 us
    all_gather x1, waiting for transfers between devices, shards(): lax.all_gather(first.astype(jnp.bfloat16), 'head', axis=0, tiled=True)  35.1 us
    all_gather x1, blocking collectives, shards(): lax.all_gather(starts[2], 'dp', axis=1, tiled=True)  31.2 us
  transfers between devices with their start and end apart: 23, of which 15 were waited for; matrix products, arithmetic and copies ran while one was open for 21% of the time, Pallas kernels for 0%

profile of v1, /device:TPU:0, one launch (start us, length us, event | category | flops | bytes accessed | tf_op | source)
XLA Modules:
  0.0 1168.1 jit_solution(6152565567794218936)
XLA Ops:
  13.5 35.1 %all-gather.5.cloned.1.call-done = bf16[4096,512]{0,1:T(8,128)(2,1)} async-done(((bf16[1024,512]{0,1:T(8,128)(2,1)}), bf16[4096,512]{0,1:T(8,128)(2,1)}) %all-gather.5.cloned.1.call-update) | async-done | bytes 4194320 | tf_op jit(solution)/shard_map/all_gather | solution.py:145
  48.6 6.2 convolution_convert_fusion.2
  54.8 4.8 copy.76
  59.6 3.3 copy.103
  65.1 40.1 %while.22 = (s32[]{:T(128)}, bf16[8,512,2,64]{1,3,2,0:T(8,128)(2,1)}, f32[8,2,512,1]{2,1,3,0:T(2,128)}, bf16[8,512,2,64]{1,3,2,0:T(8,128)(2,1)}, s32[8,512]{1,0:...) while((s32[]{:T(128)}, ...), condition=%wide.region_5.6_spmd, body=%wide.region_2.5_spmd.sunk | while | flops 140835840 | bytes 7905881 | solution.py:154
  105.2 3.5 copy.80
  113.8 3.6 all-to-all-start
  118.9 17.6 %all_gather.19 = bf16[512,512]{1,0:T(8,128)(2,1)} all-gather(bf16[128,512]{1,0:T(8,128)(2,1)S(1)} %convert_element_type.448), channel_id=1, replica_groups=mesh['dp'=8,'head'=4] {'head'}, dimensions={0}, use_global_device_ids=true | all-gather | bytes 655360 | tf_op jit(solution)/shard_map/all_gather | solution.py:157
  140.3 8.4 multiply_convert_fusion.2
  148.7 18.5 %all-gather.9.cloned.1.call-done = bf16[512,2048]{0,1:T(8,128)(2,1)} async-done(((bf16[512,64]{0,1:T(8,128)(2,1)}), bf16[512,2048]{0,1:T(8,128)(2,1)}) %all-gather.9.cloned.1.call-update) | async-done | bytes 2097168 | tf_op jit(solution)/shard_map/all_gather | solution.py:164
  167.2 8.4 multiply_convert_fusion.1
  175.7 4.2 fusion.272
  190.0 4.2 all-to-all-start.1
  197.5 11.2 all-to-all-done.1
  216.5 82.0 %while.23 = (s32[]{:T(128)}, bf16[8,512,2,3,64]{1,4,2,3,0:T(8,128)(2,1)}, bf16[8,512,2,64]{1,3,2,0:T(8,128)(2,1)}, s32[8,512]{1,0:T(8,128)}, bf16[8,512,2,64]{1,...) while((s32[]{:T(128)}, ...), condition=%wide.region_12.13_spmd, body=%wide.region_10.12_spmd.sunk | while | flops 342031360 | bytes 18380900 | solution.py:206
  298.4 3.7 copy.90
  309.2 7.4 fusion.267
  316.9 6.8 convolution_bitcast_fusion
  323.7 6.1 all_to_all.47
  329.8 4.6 copy.91
  334.4 4.8 all-to-all-start.2
  339.8 40.4 %all-reduce.14.cloned.1.call-done = (bf16[128,512]{1,0:T(8,128)(2,1)}, bf16[512,384]{1,0:T(8,128)(2,1)}) async-done(((bf16[128,512]{1,0:T(8,128)(2,1)}, bf16[512,384]{1,0:T(8,128)(2,1)}), (bf16[128,512]{1,0:T(8,128)(2,1)}, bf16[512,384]{1,0:T(8,128)(2,1)})) %all-reduce.14.cloned.1.call-update) | async-done | bytes 524304 | tf_op jit(solution)/shard_map/psum | solution.py:222
  388.9 12.2 %all-gather.11.cloned.1.call-done = bf16[512,1536]{1,0:T(8,128)(2,1)} async-done(((bf16[512,384]{1,0:T(8,128)(2,1)}), bf16[512,1536]{1,0:T(8,128)(2,1)}) %all-gather.11.cloned.1.call-update) | async-done | bytes 1572880 | tf_op jit(solution)/shard_map/all_gather | solution.py:212
  401.1 6.1 fusion.273
  413.7 130.7 %reduce-scatter.6.cloned.1.call-done = f32[512,64]{0,1:T(8,128)} async-done(((f32[512,2048]{0,1:T(8,128)}), f32[512,64]{0,1:T(8,128)}) %reduce-scatter.6.cloned.1.call-update) | async-done | bytes 131088 | tf_op jit(solution)/shard_map/reduce_scatter | solution.py:187
  546.0 137.6 %reduce-scatter.8.cloned.1.call-done = f32[512,64]{0,1:T(8,128)} async-done(((f32[512,2048]{0,1:T(8,128)}), f32[512,64]{0,1:T(8,128)}) %reduce-scatter.8.cloned.1.call-update) | async-done | bytes 131088 | tf_op jit(solution)/shard_map/reduce_scatter | solution.py:188
  685.3 4.0 maximum_bitcast_fusion
  691.7 37.2 %all-reduce = (f32[4,3]{1,0:T(4,128)S(1)}, f32[4,512]{1,0:T(4,128)}) all-reduce(f32[4,3]{1,0:T(4,128)} %pad_maximum_fusion.1, f32[4,512]{1,0:T(4,128)} %pad_maximum_fusion), channel_id=1, replica_groups=mesh['dp'=8,'head'=4] {'dp','head'}, use_global_device_ids=true, to_apply=%region_32.33 | all-reduce | flops 2060 | bytes 16480 | tf_op jit(solution)/shard_map/psum | solution.py:236
  742.5 31.2 %all_gather.23 = bf16[512,512]{0,1:T(8,128)(2,1)S(1)} all-gather(bf16[512,64]{0,1:T(8,128)(2,1)S(1)} %get-tuple-element.243), channel_id=1, replica_groups=mesh['dp'=8,'head'=4] {'dp'}, dimensions={1}, use_global_device_ids=true | all-gather | bytes 589824 | tf_op jit(solution)/shard_map/all_gather | solution.py:249
  777.9 5.7 collective-permute-done.1
  784.3 4.8 collective-permute-start.5
  791.7 4.7 collective-permute-start.6
  807.8 51.0 %all-reduce.24.cloned.1.call-done = (bf16[512,512]{1,0:T(8,128)(2,1)}, bf16[512,512]{1,0:T(8,128)(2,1)}, bf16[512,512]{1,0:T(8,128)(2,1)}, bf16[512,512]{1,0:T(8,128)(2,1)}) async-done(((bf16[512,512]{1,0:T(8,128)(2,1)}, bf16[512,512]{1,0:T(8,128)(2,1)}, bf16[512,512]{1,0:T(8,128)(2,1)}, bf16[512,512]{1,0:T(8,128)(2,1)}), (bf16[512,512]{1,0:T(8,128)(2,1)}, bf16[512,512]{1,0:T(8,128)(2,1)}, ...) | async-done | bytes 2097168 | tf_op jit(solution)/shard_map/psum | solution.py:261
  858.9 3.3 fusion.101
  864.7 3.4 fusion.96
  878.0 52.1 %all-reduce.22.cloned.1.call-done = (bf16[512,512]{1,0:T(8,128)(2,1)}, bf16[512,512]{1,0:T(8,128)(2,1)}, bf16[512,512]{1,0:T(8,128)(2,1)}, bf16[512,512]{1,0:T(8,128)(2,1)}) async-done(((bf16[512,512]{1,0:T(8,128)(2,1)}, bf16[512,512]{1,0:T(8,128)(2,1)}, bf16[512,512]{1,0:T(8,128)(2,1)}, bf16[512,512]{1,0:T(8,128)(2,1)}), (bf16[512,512]{1,0:T(8,128)(2,1)}, bf16[512,512]{1,0:T(8,128)(2,1)}, ...) | async-done | bytes 2097168 | tf_op jit(solution)/shard_map/psum | solution.py:261
  930.1 3.4 fusion.102
  935.9 3.5 fusion.97
  952.3 52.1 %all-reduce.20.cloned.1.call-done = (bf16[512,512]{1,0:T(8,128)(2,1)}, bf16[512,512]{1,0:T(8,128)(2,1)}, bf16[512,512]{1,0:T(8,128)(2,1)}, bf16[512,512]{1,0:T(8,128)(2,1)}) async-done(((bf16[512,512]{1,0:T(8,128)(2,1)}, bf16[512,512]{1,0:T(8,128)(2,1)}, bf16[512,512]{1,0:T(8,128)(2,1)}, bf16[512,512]{1,0:T(8,128)(2,1)}), (bf16[512,512]{1,0:T(8,128)(2,1)}, bf16[512,512]{1,0:T(8,128)(2,1)}, ...) | async-done | bytes 2097168 | tf_op jit(solution)/shard_map/psum | solution.py:261
  1004.4 3.4 fusion.103
  1010.3 3.5 fusion.98
  1023.4 6.8 add_convert_fusion
  1033.1 42.2 %all-reduce.18.cloned.1.call-done = (bf16[512,512]{1,0:T(8,128)(2,1)}, bf16[512,512]{1,0:T(8,128)(2,1)}, bf16[512,512]{1,0:T(8,128)(2,1)}, bf16[512,512]{1,0:T(8,128)(2,1)}) async-done(((bf16[512,512]{1,0:T(8,128)(2,1)}, bf16[512,512]{1,0:T(8,128)(2,1)}, bf16[512,512]{1,0:T(8,128)(2,1)}, bf16[512,512]{1,0:T(8,128)(2,1)}), (bf16[512,512]{1,0:T(8,128)(2,1)}, bf16[512,512]{1,0:T(8,128)(2,1)}, ...) | async-done | bytes 2097168 | tf_op jit(solution)/shard_map/psum | solution.py:261
  1075.3 3.6 fusion.104
  1081.4 3.3 fusion.99
  1094.4 3.6 fusion.53
  1102.1 44.4 %all-reduce.16.cloned.1.call-done = (bf16[512,512]{1,0:T(8,128)(2,1)}, bf16[512,512]{1,0:T(8,128)(2,1)}, bf16[512,512]{1,0:T(8,128)(2,1)}, bf16[512,512]{1,0:T(8,128)(2,1)}) async-done(((bf16[512,512]{1,0:T(8,128)(2,1)}, bf16[512,512]{1,0:T(8,128)(2,1)}, bf16[512,512]{1,0:T(8,128)(2,1)}, bf16[512,512]{1,0:T(8,128)(2,1)}), (bf16[512,512]{1,0:T(8,128)(2,1)}, bf16[512,512]{1,0:T(8,128)(2,1)}, ...) | async-done | bytes 2097168 | tf_op jit(solution)/shard_map/psum | solution.py:261
  1146.5 3.3 fusion.113
  (378 shorter events, 287.4 us)
Async XLA Ops:
  7.2 41.4 %all-gather.5.cloned.1.call-start = ((), (), s32[]{:S(2)}) async-start(), calls=%async_computation.6 | async-start | bytes 5242880 | tf_op jit(solution)/shard_map/all_gather | solution.py:145
  11.3 128.7 %all-gather.7.cloned.1.call-start = ((), (), s32[]{:S(2)}) async-start(), calls=%async_computation.7 | async-start | bytes 2162688 | tf_op jit(solution)/shard_map/all_gather | solution.py:163
  12.0 155.2 %all-gather.9.cloned.1.call-start = ((), (), s32[]{:S(2)}) async-start(), calls=%async_computation.8 | async-start | bytes 2162688 | tf_op jit(solution)/shard_map/all_gather | solution.py:164
  12.8 42.0 %copy-start.10 = (bf16[512,384]{1,0:T(8,128)(2,1)}, bf16[512,384]{1,0:T(8,128)(2,1)S(1)}, u32[]{:S(2)}) copy-start(bf16[512,384]{1,0:T(8,128)(2,1)S(1)} %convert_element_type.446) | copy-start | bytes 1179652
  105.2 6.1 copy-start.4
  105.2 6.1 copy-start.5
  111.2 6.2 copy-start.31
  113.8 22.7 %all-to-all-start = ((bf16[4,1024,128]{1,2,0:T(8,128)(2,1)}), bf16[4,1024,128]{1,2,0:T(8,128)(2,1)S(1)}, u32[]{:S(2)}, u32[]{:S(2)}) async-start(bf16[4,1024,128]{1,2,0:T(8,128)(2,1)} %copy.81), calls=%async_computation | async-start | bytes 2097152 | tf_op jit(solution)/shard_map/all_to_all | solution.py:156
  139.6 43.2 %copy-start = (f32[1024,512]{0,1:T(8,128)}, f32[1024,512]{0,1:T(8,128)S(1)}, u32[]{:S(2)}) copy-start(f32[1024,512]{0,1:T(8,128)S(1)} %get-tuple-element.263) | copy-start | bytes 6291460
  167.2 8.4 copy-start.49
  175.6 4.2 copy-start.51
  190.0 18.8 %all-to-all-start.1 = ((bf16[1024,4,128]{0,2,1:T(8,128)(2,1)}), bf16[1024,4,128]{0,2,1:T(8,128)(2,1)}, u32[]{:S(2)}, u32[]{:S(2)}) async-start(bf16[1024,4,128]{0,2,1:T(8,128)(2,1)} %bitcast.309), calls=%async_computation.1 | async-start | bytes 2097152 | tf_op jit(solution)/shard_map/all_to_all | solution.py:198
  194.2 114.4 %reduce-scatter.4.cloned.1.call-start = ((), (), s32[]{:S(2)}) async-start(), calls=%async_computation.10 | async-start | bytes 655360 | tf_op jit(solution)/shard_map/reduce_scatter | solution.py:202
  197.1 183.2 %all-reduce.14.cloned.1.call-start = ((), (), s32[]{:S(2)}) async-start(), calls=%async_computation.13 | async-start | bytes 1048576 | tf_op jit(solution)/shard_map/psum | solution.py:222
  308.6 92.5 %all-gather.11.cloned.1.call-start = ((), (), s32[]{:S(2)}) async-start(), calls=%async_computation.9 | async-start | bytes 1966080 | tf_op jit(solution)/shard_map/all_gather | solution.py:212
  309.2 235.2 %reduce-scatter.6.cloned.1.call-start = ((), (), s32[]{:S(2)}) async-start(), calls=%async_computation.11 | async-start | bytes 4325376 | tf_op jit(solution)/shard_map/reduce_scatter | solution.py:187
  316.6 367.0 %reduce-scatter.8.cloned.1.call-start = ((), (), s32[]{:S(2)}) async-start(), calls=%async_computation.12 | async-start | bytes 4325376 | tf_op jit(solution)/shard_map/reduce_scatter | solution.py:188
  334.4 50.4 %copy-start.12 = (f32[128,512]{1,0:T(8,128)S(1)}, f32[128,512]{1,0:T(8,128)}, u32[]{:S(2)}) copy-start(f32[128,512]{1,0:T(8,128)} %param.27) | copy-start | bytes 786436
  334.4 66.8 %all-to-all-start.2 = ((bf16[4,1024,384]{1,2,0:T(8,128)(2,1)}), bf16[4,1024,384]{1,2,0:T(8,128)(2,1)}, u32[]{:S(2)}, u32[]{:S(2)}) async-start(bf16[4,1024,384]{1,2,0:T(8,128)(2,1)} %copy.91), calls=%async_computation.2 | async-start | bytes 6291456 | tf_op jit(solution)/shard_map/all_to_all | solution.py:211
  339.2 519.7 %all-reduce.24.cloned.1.call-start = ((), (), s32[]{:S(2)}) async-start(), calls=%async_computation.18 | async-start | bytes 4194304 | tf_op jit(solution)/shard_map/psum | solution.py:261
  410.1 329.8 %copy-start.8 = (bf16[512,384]{1,0:T(8,128)(2,1)S(1)}, bf16[512,384]{1,0:T(8,128)(2,1)}, u32[]{:S(2)}) copy-start(bf16[512,384]{1,0:T(8,128)(2,1)} %get-tuple-element.220) | copy-start | bytes 1179652
  732.3 9.6 copy-start.23
  732.3 9.6 copy-start.24
  735.2 41.3 %collective-permute-start = (bf16[512,64]{0,1:T(8,128)(2,1)S(1)}, bf16[512,64]{0,1:T(8,128)(2,1)S(1)}, u32[]{:S(2)}, u32[]{:S(2)}) collective-permute-start(bf16[512,64]{0,1:T(8,128)(2,1)S(1)} %get-tuple-element.241), channel_id=1, source_target_pairs={{0,4},{4,8},{8,12},{12,16},{16,20},{20,24},{24,28},{28,0},{1,5},{5... | collective-permute-start | bytes 196616 | tf_op jit(solution)/shard_map/ppermute | solution.py:36
  737.8 46.5 %collective-permute-start.4 = (bf16[512,64]{0,1:T(8,128)(2,1)S(1)}, bf16[512,64]{0,1:T(8,128)(2,1)S(1)}, u32[]{:S(2)}, u32[]{:S(2)}) collective-permute-start(bf16[512,64]{0,1:T(8,128)(2,1)S(1)} %get-tuple-element.241), channel_id=1, source_target_pairs={{4,0},{8,4},{12,8},{16,12},{20,16},{24,20},{28,24},{0,28},{5,1},{9... | collective-permute-start | bytes 196616 | tf_op jit(solution)/shard_map/ppermute | solution.py:38
  741.2 36.7 %copy-start.16 = (f32[512,384]{1,0:T(8,128)}, f32[512,384]{1,0:T(8,128)S(1)}, u32[]{:S(2)}) copy-start(f32[512,384]{1,0:T(8,128)S(1)} %fusion.175) | copy-start | bytes 2359300
  775.8 7.7 copy-start.13
  775.8 7.7 copy-start.30
  776.5 7.0 collective-permute-start.1
  783.6 7.0 collective-permute-start.2
  783.6 87.0 %copy-start.33 = (f32[128,512]{1,0:T(8,128)}, f32[128,512]{1,0:T(8,128)S(1)}, u32[]{:S(2)}) copy-start(f32[128,512]{1,0:T(8,128)S(1)} %fusion.221) | copy-start | bytes 786436
  784.3 7.4 collective-permute-start.5
  790.5 7.0 collective-permute-start.3
  791.7 10.3 collective-permute-start.6
  807.6 122.5 %all-reduce.22.cloned.1.call-start = ((), (), s32[]{:S(2)}) async-start(), calls=%async_computation.17 | async-start | bytes 4194304 | tf_op jit(solution)/shard_map/psum | solution.py:261
  877.9 126.5 %all-reduce.20.cloned.1.call-start = ((), (), s32[]{:S(2)}) async-start(), calls=%async_computation.16 | async-start | bytes 4194304 | tf_op jit(solution)/shard_map/psum | solution.py:261
  952.2 123.1 %all-reduce.18.cloned.1.call-start = ((), (), s32[]{:S(2)}) async-start(), calls=%async_computation.15 | async-start | bytes 4194304 | tf_op jit(solution)/shard_map/psum | solution.py:261
  1010.3 5.9 copy-start.22
  1021.8 8.4 copy-start.9
  1023.1 123.4 %all-reduce.16.cloned.1.call-start = ((), (), s32[]{:S(2)}) async-start(), calls=%async_computation.14 | async-start | bytes 4194304 | tf_op jit(solution)/shard_map/psum | solution.py:261
  1081.4 5.8 copy-start.20
  1097.9 48.6 %copy-start.42 = (bf16[512,512]{0,1:T(8,128)(2,1)S(1)}, bf16[512,512]{0,1:T(8,128)(2,1)}, u32[]{:S(2)}) copy-start(bf16[512,512]{0,1:T(8,128)(2,1)} %fusion.104) | copy-start | bytes 1572868
  1100.9 48.9 %copy-start.43 = (bf16[512,512]{0,1:T(8,128)(2,1)S(1)}, bf16[512,512]{0,1:T(8,128)(2,1)}, u32[]{:S(2)}) copy-start(bf16[512,512]{0,1:T(8,128)(2,1)} %fusion.99) | copy-start | bytes 1572868
  1101.5 50.7 %copy-start.34 = (f32[4,512]{1,0:T(4,128)}, f32[4,512]{1,0:T(4,128)S(1)}, u32[]{:S(2)}) copy-start(f32[4,512]{1,0:T(4,128)S(1)} %get-tuple-element.246) | copy-start | bytes 24580
  1149.8 5.7 copy-start.18
  1149.8 5.7 copy-start.32
  1152.2 6.1 copy-start.15
  1153.9 4.4 copy-start.50
  (27 other events, 66.1 us)
Sparse Core Ops, SparseCore 0:
  11.4 37.1 all-gather.4
  52.0 56.3 all-gather.6
  111.9 55.3 all-gather.8
  197.8 21.9 reduce-scatter.3
  308.7 71.4 all-reduce.13
  382.2 18.8 all-gather.10
  403.4 140.9 reduce-scatter.5
  546.7 136.9 reduce-scatter.7
  807.7 51.1 all-reduce.23
  878.0 51.9 all-reduce.21
  952.3 52.0 all-reduce.19
  1023.3 51.9 all-reduce.17
  1094.5 52.0 all-reduce.15
